TPU v7x, 256 devices: a whole 4x4x8 slice. The times are simulated.
256 devices in a mesh: aux: 2 (over core), row: 8 (over z), col: 16 (over x, y).
Axes of the slice: x: 4, y: 4, z: 8, core: 2. Of those that a mesh axis runs over, the one named last changes fastest.
Arguments:
- coulomb: bfloat16 [64, 2048, 2048], P('aux', 'row', 'col'), may hold values from -6 to 6
- occupied: bfloat16 [2048, 2048], P('row'), may hold values from -0.125 to 0.125
- virtual: bfloat16 [2048, 2048], P('row'), may hold values from -0.125 to 0.125
- tile_mask: int32 [16, 16], replicated, may hold values 0 or 1
Outputs:
- chi: float32 [64, 64], P('aux')
All inputs are finite; a program needn't handle non-finite values.
Results may differ from a plain program's by a relative error of at most 0.0042.
Values may be sent and summed in bfloat16 or wider, within the bound.
A program may use at most 128 MiB of HBM per device.

v0:
```python
import jax
import jax.numpy as jnp
from jax import lax
from jax.sharding import PartitionSpec as P

NAO = 2048
TILE = 128


def swapped(value, axis, apart):
    mask = 2**apart
    pairs = [(source, source ^ mask) for source in range(lax.axis_size(axis))]
    return lax.ppermute(value, axis, pairs)


def shards(coulomb, occupied, virtual, tile_mask):
    rows = lax.axis_size("row")
    cols = lax.axis_size("col")
    pdev, mrow, ncol = coulomb.shape
    nao = mrow * rows
    row_idx = lax.axis_index("row")
    col_idx = lax.axis_index("col")
    aux_idx = lax.axis_index("aux")
    tiles_r = mrow // TILE
    tiles_c = ncol // TILE
    local_tiles = lax.dynamic_slice(
        tile_mask, (row_idx * tiles_r, col_idx * tiles_c), (tiles_r, tiles_c)
    )
    local_mask = jnp.repeat(jnp.repeat(local_tiles, TILE, axis=0), TILE, axis=1).astype(
        jnp.bfloat16
    )
    screened = coulomb * local_mask[None]
    moved = lax.all_to_all(screened, "row", split_axis=0, concat_axis=1, tiled=True)
    pieces = moved.shape[0]
    occ_all, virt_all = (
        lax.all_gather(occupied, "row", axis=0, tiled=True),
        lax.all_gather(virtual, "row", axis=0, tiled=True),
    )
    half = jnp.einsum("ml,pmn->pln", occ_all, moved, preferred_element_type=jnp.float32).astype(
        jnp.bfloat16
    )
    jpart = mrow // cols
    shaped = half.reshape(pieces, rows, cols, jpart, ncol)
    spread = lax.all_to_all(shaped, "col", split_axis=2, concat_axis=4, tiled=True)
    spread = spread.reshape(pieces, rows * jpart, nao)
    dressed = jnp.einsum(
        "pln,ns->pls", spread, virt_all, preferred_element_type=jnp.float32
    ).astype(jnp.bfloat16)
    layered = dressed.reshape(pieces, rows, 1, jpart, cols, ncol)
    returned = lax.all_to_all(
        lax.all_to_all(layered, "row", split_axis=1, concat_axis=0, tiled=True),
        "col",
        split_axis=4,
        concat_axis=2,
        tiled=True,
    )
    aligned = returned.reshape(pdev, mrow, ncol)
    theirs = swapped(screened, "aux", 0)
    with_mine = jnp.einsum("pls,qls->pq", aligned, screened, preferred_element_type=jnp.float32)
    with_theirs = jnp.einsum("pls,qls->pq", aligned, theirs, preferred_element_type=jnp.float32)
    first_half = jnp.where(aux_idx == 0, with_mine, with_theirs)
    second_half = jnp.where(aux_idx == 0, with_theirs, with_mine)
    partial_chi = jnp.concatenate([first_half, second_half], axis=1)
    total_chi = lax.psum(partial_chi, ("row", "col"))
    return total_chi / NAO


def solution(mesh):
    placed = (P("aux", "row", "col"), P("row", None), P("row", None), P())
    return jax.shard_map(
        shards, mesh=mesh, in_specs=placed, out_specs=P("aux", None), check_vma=False
    )
```

profile of v0, /device:TPU:0, one launch (start us, length us, event | category | flops | bytes accessed | tf_op | source)
XLA Modules:
  0.0 1038.5 jit_solution(6755601709993652313)
XLA Ops:
  6.5 0.7 all-gather.3.cloned.1.call-update
  7.3 0.0 all-gather.5.cloned.1.call-start
  7.3 0.7 all-gather.5.cloned.1.call-update
  8.0 0.9 fusion.13
  8.9 0.1 broadcast_bitcast_fusion
  9.0 2.8 copy_multiply_fusion
  11.7 0.8 copy.15
  12.6 80.1 %all_to_all.66 = bf16[32,256,128]{2,1,0:T(8,128)(2,1)} all-to-all(bf16[32,256,128]{2,1,0:T(8,128)(2,1)S(1)} %copy.15), channel_id=1, replica_groups=mesh['aux'=2,'row'=8,'col'=16] {'row'}, dimensions={0} | all-to-all | bytes 4194304 | tf_op jit(solution)/shard_map/all_to_all | solution.py:33
  92.7 4.5 copy.16
  97.2 4.2 all_to_all.51
  101.4 45.5 %all-gather.3.cloned.1.call-done = bf16[2048,2048]{1,0:T(8,128)(2,1)} async-done(((bf16[256,2048]{1,0:T(8,128)(2,1)}), bf16[2048,2048]{1,0:T(8,128)(2,1)}) %all-gather.3.cloned.1.call-update) | async-done | bytes 8388624 | tf_op jit(solution)/shard_map/all_gather | solution.py:36
  146.9 9.8 fusion.10
  156.7 3.9 copy.17
  160.6 2.2 copy.18
  162.8 35.3 %all_to_all.67 = bf16[4,8,16,16,128]{4,3,1,0,2:T(8,128)(2,1)S(1)} all-to-all(bf16[4,8,16,16,128]{4,3,1,0,2:T(8,128)(2,1)S(1)} %copy.18), channel_id=1, replica_groups=mesh['aux'=2,'row'=8,'col'=16] {'col'}, dimensions={2} | all-to-all | bytes 4194304 | tf_op jit(solution)/shard_map/all_to_all | solution.py:44
  198.1 3.7 copy.19
  201.9 4.2 reshape.35
  206.0 35.8 %all-gather.5.cloned.1.call-done = bf16[2048,2048]{1,0:T(8,128)(2,1)} async-done(((bf16[256,2048]{1,0:T(8,128)(2,1)}), bf16[2048,2048]{1,0:T(8,128)(2,1)}) %all-gather.5.cloned.1.call-update) | async-done | bytes 8388624 | tf_op jit(solution)/shard_map/all_gather | solution.py:37
  241.9 8.5 fusion.7
  250.4 0.6 copy.23
  251.0 0.6 copy.20
  251.6 55.3 %all_to_all.68 = bf16[4,8,1,16,16,128]{5,4,3,0,2,1:T(8,128)(2,1)S(1)} all-to-all(bf16[4,8,1,16,16,128]{5,4,3,0,2,1:T(8,128)(2,1)S(1)} %copy.20), channel_id=1, replica_groups=mesh['aux'=2,'row'=8,'col'=16] {'row'}, dimensions={1} | all-to-all | bytes 4194304 | tf_op jit(solution)/shard_map/all_to_all | solution.py:51
  306.9 1.8 copy.21
  308.8 6.9 all-to-all-start.3
  315.6 0.1 collective-permute-start
  315.7 27.9 %all-to-all-done.3 = bf16[32,1,1,16,16,128]{5,3,0,2,1,4:T(8,128)(2,1)} async-done(((bf16[32,1,1,16,16,128]{5,3,0,2,1,4:T(8,128)(2,1)}), bf16[32,1,1,16,16,128]{5,3,0,2,1,4:T(8,128)(2,1)}, u32[]{:S(2)}, u32[]{:S(2)}) %all-to-all-start.3) | async-done | bytes 2097184 | tf_op jit(solution)/shard_map/all_to_all | solution.py:50
  343.7 2.1 copy.22
  345.8 0.7 convolution_bitcast_fusion.1
  346.5 2.3 broadcast_select_fusion.1
  348.8 0.1 pad_maximum_fusion
  348.9 682.2 %psum.7 = f32[32,64]{1,0:T(8,128)S(1)} all-reduce(f32[32,64]{1,0:T(8,128)S(1)} %pad_maximum_fusion), channel_id=1, replica_groups=mesh['aux'=2,'row'=8,'col'=16] {'row','col'}, use_global_device_ids=true, to_apply=%region_0.1 | all-reduce | flops 2048 | bytes 16384 | tf_op jit(solution)/shard_map/psum | solution.py:64
  1031.1 0.6 broadcast_multiply_fusion
  (2 shorter events, 0.0 us)
Async XLA Ops:
  6.5 140.3 %all-gather.3.cloned.1.call-start = ((), (), s32[]{:S(2)}) async-start(), calls=%async_computation.4 | async-start | bytes 9437184 | tf_op jit(solution)/shard_map/all_gather | solution.py:36
  7.3 234.6 %all-gather.5.cloned.1.call-start = ((), (), s32[]{:S(2)}) async-start(), calls=%async_computation.5 | async-start | bytes 9437184 | tf_op jit(solution)/shard_map/all_gather | solution.py:37
  308.8 34.9 %all-to-all-start.3 = ((bf16[32,1,1,16,16,128]{5,3,0,2,1,4:T(8,128)(2,1)}), bf16[32,1,1,16,16,128]{5,3,0,2,1,4:T(8,128)(2,1)}, u32[]{:S(2)}, u32[]{:S(2)}) async-start(bf16[32,1,1,16,16,128]{5,3,0,2,1,4:T(8,128)(2,1)} %copy.21), calls=%async_computation.3 | async-start | bytes 4194304 | tf_op jit(solution)/shard_map/all_to_all | solution.py:50
  315.6 30.8 %collective-permute-start = (bf16[32,256,128]{2,0,1:T(8,128)(2,1)S(1)}, bf16[32,256,128]{2,0,1:T(8,128)(2,1)}, u32[]{:S(2)}, u32[]{:S(2)}) collective-permute-start(bf16[32,256,128]{2,0,1:T(8,128)(2,1)S(1)} %copy_multiply_fusion), channel_id=1, source_target_pairs={{0,128},{128,0},{1,129},{129,1},{2,130},{130,2},{3,131},{131,3},{4... | collective-permute-start | bytes 6291464 | tf_op jit(solution)/shard_map/ppermute | solution.py:13
Sparse Core Ops, SparseCore 0:
  9.1 137.6 all-gather.2
  148.7 93.1 all-gather.4
where the time goes:
time: 1040 us
  blocking collectives  853 us (82%)
  waiting for transfers between devices  111 us (11%)
  local copies, waits for them, and re-layouts  28.8 us (3%)
  matrix products  21.3 us (2%)
  between operations  13.5 us (1%)
    psum x1, blocking collectives, shards(): total_chi = lax.psum(partial_chi, ('row', 'col'))  682 us
    all_to_all x1, blocking collectives, shards(): lax.all_to_all(screened, 'row', split_axis=0, concat_axis=1, tiled=True)  80.1 us
    all_to_all x1, blocking collectives, shards(): lax.all_to_all(layered, 'row', split_axis=1, concat_axis=0, tiled=True)  55.3 us
    all_gather x1, waiting for transfers between devices, shards(): lax.all_gather(occupied, 'row', axis=0, tiled=True)  45.5 us
    all_gather x1, waiting for transfers between devices, shards(): lax.all_gather(virtual, 'row', axis=0, tiled=True)  35.8 us
    all_to_all x1, blocking collectives, shards(): lax.all_to_all(shaped, 'col', split_axis=2, concat_axis=4, tiled=True)  35.3 us
    all_to_all x1, waiting for transfers between devices, shards(): lax.all_to_all(lax.all_to_all(layered, 'row', split_axis=1, concat_axis=0...  27.9 us
  transfers between devices with their start and end apart: 4, of which 3 were waited for; matrix products, arithmetic and copies ran while one was open for 3% of the time, Pallas kernels for 0%

commit v1 on v0

--- a/solution.py
+++ b/solution.py
@@ -5,6 +5,12 @@
 
 NAO = 2048
 TILE = 128
+
+
+def press_trails(a0):
+    top = lax.psum(a0, "row")
+    high = lax.psum(top, "col")
+    return high
 
 
 def swapped(value, axis, apart):
@@ -61,7 +67,7 @@
     first_half = jnp.where(aux_idx == 0, with_mine, with_theirs)
     second_half = jnp.where(aux_idx == 0, with_theirs, with_mine)
     partial_chi = jnp.concatenate([first_half, second_half], axis=1)
-    total_chi = lax.psum(partial_chi, ("row", "col"))
+    total_chi = press_trails(partial_chi)
     return total_chi / NAO
 
 

time: 1040 us -> 455 us (0.44)
  blocking collectives: 853 us -> 269 us
    psum x1 -> x2, blocking collectives: 682 us -> 98.3 us  [the longest x1 71.1 us: press_trails(): high = lax.psum(top, 'col')]
  transfers between devices with their start and end apart: 4 -> 4, of which waited for: 3 -> 3; matrix products, arithmetic and copies ran while one was open for 3% -> 8% of each run, Pallas kernels for 0% -> 0%
where the time goes in v1:
time: 455 us
  blocking collectives  269 us (59%)
  waiting for transfers between devices  111 us (24%)
  local copies, waits for them, and re-layouts  28.8 us (6%)
  matrix products  21.3 us (5%)
  between operations  13.5 us (3%)
  starting transfers between devices  6.99 us (2%)
    all_to_all x1, blocking collectives, shards(): lax.all_to_all(screened, 'row', split_axis=0, concat_axis=1, tiled=True)  80.1 us
    psum x1, blocking collectives, press_trails(): high = lax.psum(top, 'col')  71.1 us
    all_to_all x1, blocking collectives, shards(): lax.all_to_all(layered, 'row', split_axis=1, concat_axis=0, tiled=True)  55.3 us
    all_gather x1, waiting for transfers between devices, shards(): lax.all_gather(occupied, 'row', axis=0, tiled=True)  45.5 us
    all_gather x1, waiting for transfers between devices, shards(): lax.all_gather(virtual, 'row', axis=0, tiled=True)  35.7 us
    all_to_all x1, blocking collectives, shards(): lax.all_to_all(shaped, 'col', split_axis=2, concat_axis=4, tiled=True)  35.4 us
    all_to_all x1, waiting for transfers between devices, shards(): lax.all_to_all(lax.all_to_all(layered, 'row', split_axis=1, concat_axis=0...  27.9 us
    psum x1, blocking collectives, press_trails(): top = lax.psum(a0, 'row')  27.2 us
  transfers between devices with their start and end apart: 4, of which 3 were waited for; matrix products, arithmetic and copies ran while one was open for 8% of the time, Pallas kernels for 0%

profile of v1, /device:TPU:0, one launch (start us, length us, event | category | flops | bytes accessed | tf_op | source)
XLA Modules:
  0.0 454.6 jit_solution(17523791207048425931)
XLA Ops:
  6.5 0.7 all-gather.3.cloned.1.call-update
  7.3 0.7 all-gather.5.cloned.1.call-update
  8.0 0.9 fusion.13
  8.9 0.1 broadcast_bitcast_fusion
  9.0 2.8 copy_multiply_fusion
  11.7 0.8 copy.15
  12.6 80.1 %all_to_all.66 = bf16[32,256,128]{2,1,0:T(8,128)(2,1)} all-to-all(bf16[32,256,128]{2,1,0:T(8,128)(2,1)S(1)} %copy.15), channel_id=1, replica_groups=mesh['aux'=2,'row'=8,'col'=16] {'row'}, dimensions={0} | all-to-all | bytes 4194304 | tf_op jit(solution)/shard_map/all_to_all | solution.py:39
  92.7 4.5 copy.16
  97.2 4.2 all_to_all.51
  101.4 45.5 %all-gather.3.cloned.1.call-done = bf16[2048,2048]{1,0:T(8,128)(2,1)} async-done(((bf16[256,2048]{1,0:T(8,128)(2,1)}), bf16[2048,2048]{1,0:T(8,128)(2,1)}) %all-gather.3.cloned.1.call-update) | async-done | bytes 8388624 | tf_op jit(solution)/shard_map/all_gather | solution.py:42
  146.9 9.8 %fusion.10 = bf16[4,2048,128]{1,2,0:T(8,128)(2,1)} fusion(bf16[4,2048,128]{1,2,0:T(8,128)(2,1)} %all_to_all.51, bf16[2048,2048]{1,0:T(8,128)(2,1)} %all-gather.3.cloned.1.call-done), kind=kOutput, calls=%fused_computation.6 | convolution fusion | flops 4296015872 | bytes 12582912 | tf_op jit(solution)/shard_map/ml,pmn->pln/dot_general | solution.py:45
  156.7 3.9 copy.17
  160.6 2.2 copy.18
  162.8 35.4 %all_to_all.67 = bf16[4,8,16,16,128]{4,3,1,0,2:T(8,128)(2,1)S(1)} all-to-all(bf16[4,8,16,16,128]{4,3,1,0,2:T(8,128)(2,1)S(1)} %copy.18), channel_id=1, replica_groups=mesh['aux'=2,'row'=8,'col'=16] {'col'}, dimensions={2} | all-to-all | bytes 4194304 | tf_op jit(solution)/shard_map/all_to_all | solution.py:50
  198.2 3.7 copy.19
  202.0 4.2 reshape.35
  206.2 35.7 %all-gather.5.cloned.1.call-done = bf16[2048,2048]{1,0:T(8,128)(2,1)} async-done(((bf16[256,2048]{1,0:T(8,128)(2,1)}), bf16[2048,2048]{1,0:T(8,128)(2,1)}) %all-gather.5.cloned.1.call-update) | async-done | bytes 8388624 | tf_op jit(solution)/shard_map/all_gather | solution.py:43
  241.9 8.5 %fusion.7 = bf16[4,128,2048]{2,1,0:T(8,128)(2,1)S(1)} fusion(bf16[4,128,2048]{2,1,0:T(8,128)(2,1)} %reshape.35, bf16[2048,2048]{1,0:T(8,128)(2,1)} %all-gather.5.cloned.1.call-done), kind=kOutput, calls=%fused_computation.5 | convolution fusion | flops 4296015872 | bytes 12582912 | tf_op jit(solution)/shard_map/pln,ns->pls/dot_general | solution.py:52
  250.4 0.6 copy.23
  251.0 0.6 copy.20
  251.6 55.3 %all_to_all.68 = bf16[4,8,1,16,16,128]{5,4,3,0,2,1:T(8,128)(2,1)S(1)} all-to-all(bf16[4,8,1,16,16,128]{5,4,3,0,2,1:T(8,128)(2,1)S(1)} %copy.20), channel_id=1, replica_groups=mesh['aux'=2,'row'=8,'col'=16] {'row'}, dimensions={1} | all-to-all | bytes 4194304 | tf_op jit(solution)/shard_map/all_to_all | solution.py:57
  306.9 1.8 copy.21
  308.8 6.9 %all-to-all-start.3 = ((bf16[32,1,1,16,16,128]{5,3,0,2,1,4:T(8,128)(2,1)}), bf16[32,1,1,16,16,128]{5,3,0,2,1,4:T(8,128)(2,1)}, u32[]{:S(2)}, u32[]{:S(2)}) async-start(bf16[32,1,1,16,16,128]{5,3,0,2,1,4:T(8,128)(2,1)} %copy.21), calls=%async_computation.3 | async-start | bytes 4194304 | tf_op jit(solution)/shard_map/all_to_all | solution.py:56
  315.6 0.1 collective-permute-start
  315.7 27.9 %all-to-all-done.3 = bf16[32,1,1,16,16,128]{5,3,0,2,1,4:T(8,128)(2,1)} async-done(((bf16[32,1,1,16,16,128]{5,3,0,2,1,4:T(8,128)(2,1)}), bf16[32,1,1,16,16,128]{5,3,0,2,1,4:T(8,128)(2,1)}, u32[]{:S(2)}, u32[]{:S(2)}) %all-to-all-start.3) | async-done | bytes 2097184 | tf_op jit(solution)/shard_map/all_to_all | solution.py:56
  343.7 2.1 copy.22
  345.8 0.7 convolution_bitcast_fusion.1
  346.5 2.3 broadcast_select_fusion.1
  348.8 0.1 pad_maximum_fusion
  348.9 27.2 %psum.14 = f32[32,64]{1,0:T(8,128)S(1)} all-reduce(f32[32,64]{1,0:T(8,128)S(1)} %pad_maximum_fusion), channel_id=1, replica_groups=mesh['aux'=2,'row'=8,'col'=16] {'row'}, use_global_device_ids=true, to_apply=%region_0.1 | all-reduce | flops 2048 | bytes 16384 | tf_op jit(solution)/shard_map/psum | solution.py:11
  376.1 71.1 %psum.15 = f32[32,64]{1,0:T(8,128)S(1)} all-reduce(f32[32,64]{1,0:T(8,128)S(1)} %psum.14), channel_id=1, replica_groups=mesh['aux'=2,'row'=8,'col'=16] {'col'}, use_global_device_ids=true, to_apply=%region_1.2 | all-reduce | flops 2048 | bytes 16384 | tf_op jit(solution)/shard_map/psum | solution.py:12
  447.1 0.6 broadcast_multiply_fusion
  (3 shorter events, 0.0 us)
Async XLA Ops:
  6.5 140.3 %all-gather.3.cloned.1.call-start = ((), (), s32[]{:S(2)}) async-start(), calls=%async_computation.4 | async-start | bytes 9437184 | tf_op jit(solution)/shard_map/all_gather | solution.py:42
  7.3 234.6 %all-gather.5.cloned.1.call-start = ((), (), s32[]{:S(2)}) async-start(), calls=%async_computation.5 | async-start | bytes 9437184 | tf_op jit(solution)/shard_map/all_gather | solution.py:43
  308.8 34.9 %all-to-all-start.3 = ((bf16[32,1,1,16,16,128]{5,3,0,2,1,4:T(8,128)(2,1)}), bf16[32,1,1,16,16,128]{5,3,0,2,1,4:T(8,128)(2,1)}, u32[]{:S(2)}, u32[]{:S(2)}) async-start(bf16[32,1,1,16,16,128]{5,3,0,2,1,4:T(8,128)(2,1)} %copy.21), calls=%async_computation.3 | async-start | bytes 4194304 | tf_op jit(solution)/shard_map/all_to_all | solution.py:56
  315.6 30.8 %collective-permute-start = (bf16[32,256,128]{2,0,1:T(8,128)(2,1)S(1)}, bf16[32,256,128]{2,0,1:T(8,128)(2,1)}, u32[]{:S(2)}, u32[]{:S(2)}) collective-permute-start(bf16[32,256,128]{2,0,1:T(8,128)(2,1)S(1)} %copy_multiply_fusion), channel_id=1, source_target_pairs={{0,128},{128,0},{1,129},{129,1},{2,130},{130,2},{3,131},{131,3},{4... | collective-permute-start | bytes 6291464 | tf_op jit(solution)/shard_map/ppermute | solution.py:19
Sparse Core Ops, SparseCore 0:
  9.1 137.6 all-gather.2
  148.7 93.1 all-gather.4
